TPU v7x, 32 devices: a whole 2x2x4 slice. The times are simulated.
32 devices in a mesh: grp: 2 (over x), tok: 4 (over y, core), feat: 4 (over z).
Axes of the slice: x: 2, y: 2, z: 4, core: 2. Of those that a mesh axis runs over, the one named last changes fastest.
Arguments:
- activations: bfloat16 [4096, 3072], P(('grp', 'tok', 'feat')), parts along dimension 0, may hold values from -6 to 6
- block_lists: int32 [2048, 4], P(('grp', 'tok', 'feat')), parts along dimension 0, may hold values from 0 to 15, as said below
- top_positions: int32 [4096, 64], P(('grp', 'tok', 'feat')), parts along dimension 0, may hold values from 0 to 2047, as said below
- enc_weight: bfloat16 [3072, 8192], P(None, ('tok', 'feat')), may hold values from -0.109375 to 0.109375
- enc_bias: float32 [8192], P(('tok', 'feat')), may hold values from -3 to 3
- dec_weight: bfloat16 [8192, 3072], P(('tok', 'feat')), may hold values from -2.5 to 2.5
- dec_bias: float32 [3072], replicated, may hold values from -6 to 6
Outputs:
- enc_grad: bfloat16 [3072, 16384], P(None, ('grp', 'tok', 'feat')), parts along dimension 1
- dec_grad: bfloat16 [16384, 3072], P(('grp', 'tok', 'feat')), parts along dimension 0
There are 2 independent parts, one for each index of `grp`. A program takes and returns all parts, laid end to end along the dimension named above; an argument that names none is the same for every part. Nothing has to cross between parts.
Inputs may be any that keep to these rules, and one draw needn't show every extreme that they name: `block_lists`: each row block names 4 different feature blocks. In the aligned blocks of 64 rows that one device holds, no feature block is named more than 24 times. In every draw one feature block is named exactly 24 times in every such block of rows. `top_positions`: the 64 entries of a token are distinct.
All inputs are finite; a program needn't handle non-finite values.
Results may differ from a plain program's by a relative error of at most 0.0058.
Values may be sent and summed in bfloat16 or wider, within the bound.
A program may use at most 128 MiB of HBM per device.

v0:
```python
import jax
import jax.numpy as jnp
from jax import lax
from jax.sharding import PartitionSpec as P


def dispatch_rows(send_x, send_rel):
    result = (
        lax.all_to_all(send_x, ("tok", "feat"), split_axis=0, concat_axis=0, tiled=True),
        lax.all_to_all(send_rel, ("tok", "feat"), split_axis=0, concat_axis=0, tiled=True),
    )
    return result


def return_partials(partial_value):
    result = lax.all_to_all(partial_value, ("tok", "feat"), split_axis=0, concat_axis=0, tiled=True)
    return result


def dispatch_errors(send_err):
    result = lax.all_to_all(send_err, ("tok", "feat"), split_axis=0, concat_axis=0, tiled=True)
    return result


def routed_plan(
    activations, block_lists, top_positions, enc_weight, enc_bias, dec_weight, dec_bias
):
    owner_count = lax.axis_size(("tok", "feat"))
    token_count, model_width = activations.shape
    block_rows, active_count = block_lists.shape
    group_rows = token_count // block_rows
    feat_block = enc_weight.shape[1]
    top_count = top_positions.shape[1]
    slot_count = max(2, 3 * token_count * active_count // (2 * group_rows * owner_count))
    per_owner = slot_count * group_rows
    buffer_rows = owner_count * per_owner
    pair_count = block_rows * active_count
    pair_ids = block_lists.reshape(pair_count)
    pair_order = jnp.arange(pair_count, dtype=jnp.int32)
    earlier = (pair_ids[:, None] == pair_ids[None, :]) & (pair_order[None, :] < pair_order[:, None])
    pair_rank = jnp.sum(earlier.astype(jnp.int32), axis=1)
    lane_index = jnp.arange(group_rows, dtype=jnp.int32)
    target = (
        (pair_ids * per_owner + pair_rank * group_rows)[:, None] + lane_index[None, :]
    ).reshape(-1)
    source = ((pair_order // active_count * group_rows)[:, None] + lane_index[None, :]).reshape(-1)
    column = jnp.repeat(pair_order % active_count, group_rows)
    slot_index = jnp.arange(buffer_rows, dtype=jnp.int32)
    hit_bool = slot_index[:, None] == target[None, :]
    hit_float = hit_bool.astype(jnp.float32)
    place_float = jnp.sum(
        hit_float.reshape(buffer_rows, block_rows, active_count, group_rows), axis=2
    ).reshape(buffer_rows, token_count)
    place = place_float.astype(jnp.bfloat16)
    filled = jnp.sum(place_float, axis=1)
    send_x = jnp.dot(place, activations, preferred_element_type=jnp.float32).astype(jnp.bfloat16)
    offsets = top_positions[source] - column[:, None] * feat_block
    offsets = jnp.where((offsets >= 0) & (offsets < feat_block), offsets, feat_block)
    rel_float = (
        jnp.dot(hit_float, offsets.astype(jnp.float32), precision=lax.Precision.HIGHEST)
        + (1.0 - filled)[:, None] * feat_block
    )
    send_rel = rel_float.astype(jnp.int32)
    recv_x, recv_rel = dispatch_rows(
        send_x.reshape(owner_count, per_owner, model_width),
        send_rel.reshape(owner_count, per_owner, top_count),
    )
    recv_x = recv_x.reshape(buffer_rows, model_width)
    recv_rel = recv_rel.reshape(buffer_rows, top_count)
    feature_iota = jnp.arange(feat_block, dtype=jnp.int32)
    mask_bool = jnp.zeros((buffer_rows, feat_block), jnp.bool_)
    for begin in range(0, top_count, 8):
        piece = recv_rel[:, begin : begin + 8]
        mask_bool = mask_bool | jnp.any(piece[:, :, None] == feature_iota[None, None, :], axis=1)
    feat_mask = mask_bool.astype(jnp.float32)
    pre_acts = jnp.dot(recv_x, enc_weight, preferred_element_type=jnp.float32) + enc_bias
    code_vals = (feat_mask * pre_acts).astype(jnp.bfloat16)
    partial_value = jnp.dot(code_vals, dec_weight, preferred_element_type=jnp.float32).astype(
        jnp.bfloat16
    )
    returned = return_partials(partial_value.reshape(owner_count, per_owner, model_width)).reshape(
        buffer_rows, model_width
    )
    summed = lax.dot_general(
        place, returned, (((0,), (0,)), ((), ())), preferred_element_type=jnp.float32
    )
    residual = (summed + dec_bias - activations.astype(jnp.float32)).astype(jnp.bfloat16)
    send_err = jnp.dot(place, residual, preferred_element_type=jnp.float32).astype(jnp.bfloat16)
    recv_err = dispatch_errors(send_err.reshape(owner_count, per_owner, model_width)).reshape(
        buffer_rows, model_width
    )
    grad_codes = lax.dot_general(
        recv_err, dec_weight, (((1,), (1,)), ((), ())), preferred_element_type=jnp.float32
    )
    grad_pre = (feat_mask * grad_codes).astype(jnp.bfloat16)
    enc_grad = lax.dot_general(
        recv_x, grad_pre, (((0,), (0,)), ((), ())), preferred_element_type=jnp.float32
    ).astype(jnp.bfloat16)
    raw_grad = lax.dot_general(
        code_vals, recv_err, (((0,), (0,)), ((), ())), preferred_element_type=jnp.float32
    )
    dec_float = dec_weight.astype(jnp.float32)
    along_coef = jnp.sum(raw_grad * dec_float, axis=1) / (
        jnp.sum(dec_float * dec_float, axis=1) + 1e-06
    )
    dec_grad = (raw_grad - along_coef[:, None] * dec_float).astype(jnp.bfloat16)
    return (enc_grad, dec_grad)


GROUP = ("tok", "feat")


def global_ids(block_lists, top_positions, feat_block):
    token_count = top_positions.shape[0]
    block_rows, active_count = block_lists.shape
    lists = jnp.repeat(block_lists, token_count // block_rows, axis=0)
    column = top_positions // feat_block
    chosen = jnp.zeros_like(top_positions)
    for k in range(active_count):
        chosen = jnp.where(column == k, lists[:, k : k + 1], chosen)
    return chosen * feat_block + top_positions % feat_block


def select_mask(rel, feat_block):
    words = feat_block // 8
    inside = (rel >= 0) & (rel < feat_block)
    word = jnp.where(inside, rel // 8, words)
    bit = jnp.left_shift(1, rel & 7)
    word_iota = jnp.arange(words, dtype=jnp.int32)
    packed = jnp.sum(
        jnp.where(word[:, :, None] == word_iota[None, None, :], bit[:, :, None], 0), axis=1
    )
    feature_iota = jnp.arange(feat_block, dtype=jnp.int32)
    spread = (word_iota[:, None] == (feature_iota // 8)[None, :]).astype(jnp.bfloat16)
    wide = jnp.dot(
        packed.astype(jnp.float32).astype(jnp.bfloat16), spread, preferred_element_type=jnp.float32
    ).astype(jnp.int32)
    return (jnp.right_shift(wide, (feature_iota & 7)[None, :]) & 1).astype(jnp.bfloat16)


def gathered_plan(
    activations, block_lists, top_positions, enc_weight, enc_bias, dec_weight, dec_bias
):
    feat_block = enc_weight.shape[1]
    ids = global_ids(block_lists, top_positions, feat_block)
    all_ids = lax.all_gather(ids, GROUP, axis=0, tiled=True)
    all_x = lax.all_gather(activations, GROUP, axis=0, tiled=True)
    mask = select_mask(all_ids - lax.axis_index(GROUP) * feat_block, feat_block)
    pre_acts = jnp.dot(all_x, enc_weight, preferred_element_type=jnp.float32) + enc_bias
    code_vals = jnp.where(mask > 0, pre_acts, 0.0).astype(jnp.bfloat16)
    partial_value = jnp.dot(code_vals, dec_weight, preferred_element_type=jnp.float32).astype(
        jnp.bfloat16
    )
    summed = lax.psum_scatter(partial_value, GROUP, scatter_dimension=0, tiled=True)
    residual = (summed.astype(jnp.float32) + dec_bias - activations.astype(jnp.float32)).astype(
        jnp.bfloat16
    )
    all_err = lax.all_gather(residual, GROUP, axis=0, tiled=True)
    grad_codes = lax.dot_general(
        all_err, dec_weight, (((1,), (1,)), ((), ())), preferred_element_type=jnp.float32
    )
    grad_pre = jnp.where(mask > 0, grad_codes, 0.0).astype(jnp.bfloat16)
    enc_grad = lax.dot_general(
        all_x, grad_pre, (((0,), (0,)), ((), ())), preferred_element_type=jnp.float32
    ).astype(jnp.bfloat16)
    raw_grad = lax.dot_general(
        code_vals, all_err, (((0,), (0,)), ((), ())), preferred_element_type=jnp.float32
    )
    dec_float = dec_weight.astype(jnp.float32)
    along_coef = jnp.sum(raw_grad * dec_float, axis=1) / (
        jnp.sum(dec_float * dec_float, axis=1) + 1e-06
    )
    dec_grad = (raw_grad - along_coef[:, None] * dec_float).astype(jnp.bfloat16)
    return (enc_grad, dec_grad)


def on_device(activations, block_lists, top_positions, *weights):
    owner_count = lax.axis_size(GROUP)
    pairs = activations.shape[0] * block_lists.shape[1]
    gathered = owner_count * activations.shape[0]
    if gathered <= 4 * pairs:
        return gathered_plan(activations, block_lists, top_positions, *weights)
    return routed_plan(activations, block_lists, top_positions, *weights)


def solution(mesh):
    placed = (
        P(("grp", "tok", "feat"), None),
        P(("grp", "tok", "feat"), None),
        P(("grp", "tok", "feat"), None),
        P(None, ("tok", "feat")),
        P(("tok", "feat")),
        P(("tok", "feat"), None),
        P(),
    )
    return jax.shard_map(
        on_device,
        mesh=mesh,
        in_specs=placed,
        out_specs=(P(None, ("grp", "tok", "feat")), P(("grp", "tok", "feat"), None)),
        check_vma=False,
    )
```

profile of v0, /device:TPU:0, one launch (start us, length us, event | category | flops | bytes accessed | tf_op | source)
XLA Modules:
  0.0 425.1 jit_solution(17819520309938272814)
XLA Ops:
  7.2 0.0 copy-start
  7.2 0.0 all-gather.3.cloned.1.call-start
  7.2 0.7 all-gather.3.cloned.1.call-update
  7.9 0.0 reduce-scatter.2.cloned.1.call-start
  8.0 0.9 copy.20
  8.9 0.2 slice_reduce_fusion.3
  9.2 0.8 fusion.11
  10.0 45.2 %all_gather.9 = s32[2048,64]{0,1:T(8,128)S(1)} all-gather(s32[128,64]{0,1:T(8,128)S(1)} %fusion.11), channel_id=1, replica_groups=mesh['grp'=2,'tok'=4,'feat'=4] {'tok','feat'}, dimensions={0}, use_global_device_ids=true | all-gather | bytes 557056 | tf_op jit(solution)/shard_map/all_gather | solution.py:146
  55.2 0.4 fusion.8
  55.6 8.9 %select_reduce_fusion = s32[2048,64]{0,1:T(8,128)S(1)} fusion(s32[2048,64]{0,1:T(8,128)S(1)} %get-tuple-element.17, s32[2048,64]{0,1:T(8,128)S(1)} %get-tuple-element.16), kind=kLoop, calls=%fused_computation | loop fusion | flops 25034752 | bytes 1572864 | tf_op jit(solution)/shard_map/reduce_sum | solution.py:130
  64.5 0.0 copy-start.6
  64.6 2.5 fusion.5
  67.0 54.2 %all-gather.3.cloned.1.call-done = bf16[2048,3072]{1,0:T(8,128)(2,1)} async-done(((bf16[128,3072]{1,0:T(8,128)(2,1)}), bf16[2048,3072]{1,0:T(8,128)(2,1)}) %all-gather.3.cloned.1.call-update) | async-done | bytes 12582928 | tf_op jit(solution)/shard_map/all_gather | solution.py:147
  121.2 0.0 copy-done
  121.2 10.1 %select_convert_fusion.1 = bf16[2048,512]{1,0:T(8,128)(2,1)S(1)} fusion(pred[2048,512]{1,0:T(32,128)(4,1)} %fusion.5, bf16[2048,3072]{1,0:T(8,128)(2,1)} %all-gather.3.cloned.1.call-done, bf16[3072,512]{1,0:T(8,128)(2,1)S(1)} %copy-done, f32[512]{0:T(512)S(1)} %copy-done.6), kind=kOutput, calls=%fused_computation.12 | convolution fusion | flops 6445596672 | bytes 18876416 | tf_op jit(solution)/shard_map/dot_general | solution.py:149
  131.3 0.0 copy-start.7
  131.3 1.3 copy-done.7
  132.6 0.0 copy-done.3
  132.6 9.7 %convolution_convert_fusion = bf16[2048,3072]{1,0:T(8,128)(2,1)} fusion(bf16[2048,512]{1,0:T(8,128)(2,1)S(1)} %select_convert_fusion.1, bf16[512,3072]{1,0:T(8,128)(2,1)S(1)} %copy-done.3), kind=kOutput, calls=%fused_computation.2 | convolution fusion | flops 6448742400 | bytes 17825792 | tf_op jit(solution)/shard_map/dot_general | solution.py:151
  142.4 0.0 reduce-scatter.2.cloned.1.call-update
  142.4 0.0 all-gather.5.cloned.1.call-start
  142.5 133.0 %reduce-scatter.2.cloned.1.call-done = bf16[128,3072]{1,0:T(8,128)(2,1)} async-done(((bf16[2048,3072]{1,0:T(8,128)(2,1)}), bf16[128,3072]{1,0:T(8,128)(2,1)}) %reduce-scatter.2.cloned.1.call-update) | async-done | bytes 786448 | tf_op jit(solution)/shard_map/reduce_scatter | solution.py:154
  275.5 0.0 copy-done.5
  275.5 2.3 subtract_convert_fusion
  277.8 0.0 all-gather.5.cloned.1.call-update
  277.8 100.1 %all-gather.5.cloned.1.call-done = bf16[2048,3072]{1,0:T(8,128)(2,1)} async-done(((bf16[128,3072]{1,0:T(8,128)(2,1)}), bf16[2048,3072]{1,0:T(8,128)(2,1)}) %all-gather.5.cloned.1.call-update) | async-done | bytes 12582928 | tf_op jit(solution)/shard_map/all_gather | solution.py:158
  377.9 23.1 %fusion.4 = bf16[3072,512]{0,1:T(8,128)(2,1)S(1)} fusion(bf16[2048,3072]{1,0:T(8,128)(2,1)} %all-gather.3.cloned.1.call-done, pred[2048,512]{1,0:T(32,128)(4,1)} %fusion.5, bf16[2048,3072]{1,0:T(8,128)(2,1)} %all-gather.5.cloned.1.call-done, bf16[512,3072]{1,0:T(8,128)(2,1)} %param.12), kind=kOutput, calls=%fused_computation.14 | convolution fusion | flops 12888571904 | bytes 32505856 | tf_op jit(solution)/shard_map/dot_general | solution.py:163
  401.0 2.8 copy.21
  403.8 11.7 %fusion.1 = (f32[512]{0:T(512)S(1)}, f32[512]{0:T(512)S(1)}, f32[512,3072]{1,0:T(8,128)S(1)}) fusion(bf16[512,3072]{1,0:T(8,128)(2,1)} %param.12, bf16[2048,512]{1,0:T(8,128)(2,1)} %copy-done.7, bf16[2048,3072]{1,0:T(8,128)(2,1)} %all-gather.5.cloned.1.call-done), kind=kOutput, calls=%fused_computation.7 | convolution fusion | flops 6450314240 | bytes 24121344 | tf_op jit(solution)/shard_map/dot_general | solution.py:166
  415.5 0.0 copy-start.1
  415.5 0.0 copy-done.4
  415.5 3.1 fusion.3
  (10 shorter events, 0.0 us)
Async XLA Ops:
  7.2 114.0 %copy-start = (bf16[3072,512]{1,0:T(8,128)(2,1)S(1)}, bf16[3072,512]{1,0:T(8,128)(2,1)}, u32[]{:S(2)}) copy-start(bf16[3072,512]{1,0:T(8,128)(2,1)} %param.10) | copy-start | bytes 9437188
  7.2 114.0 %all-gather.3.cloned.1.call-start = ((), (), s32[]{:S(2)}) async-start(), calls=%async_computation.1 | async-start | bytes 13369344 | tf_op jit(solution)/shard_map/all_gather | solution.py:147
  7.9 267.6 %reduce-scatter.2.cloned.1.call-start = ((), (), s32[]{:S(2)}) async-start(), calls=%async_computation.2 | async-start | bytes 13369344 | tf_op jit(solution)/shard_map/reduce_scatter | solution.py:154
  64.5 56.7 %copy-start.6 = (f32[512]{0:T(512)S(1)}, f32[512]{0:T(512)}, u32[]{:S(2)}) copy-start(f32[512]{0:T(512)} %param.11) | copy-start | bytes 6148
  121.2 11.4 %copy-start.3 = (bf16[512,3072]{1,0:T(8,128)(2,1)S(1)}, bf16[512,3072]{1,0:T(8,128)(2,1)}, u32[]{:S(2)}) copy-start(bf16[512,3072]{1,0:T(8,128)(2,1)} %param.12) | copy-start | bytes 9437188
  131.3 1.3 copy-start.7
  142.4 133.1 %copy-start.2 = (bf16[128,3072]{1,0:T(8,128)(2,1)S(1)}, bf16[128,3072]{1,0:T(8,128)(2,1)}, u32[]{:S(2)}) copy-start(bf16[128,3072]{1,0:T(8,128)(2,1)} %param.7) | copy-start | bytes 2359300
  142.4 133.1 %copy-start.5 = (f32[3072]{0:T(1024)S(1)}, f32[3072]{0:T(1024)}, u32[]{:S(2)}) copy-start(f32[3072]{0:T(1024)} %param.13) | copy-start | bytes 36868
  142.4 235.5 %all-gather.5.cloned.1.call-start = ((), (), s32[]{:S(2)}) async-start(), calls=%async_computation.3 | async-start | bytes 13369344 | tf_op jit(solution)/shard_map/all_gather | solution.py:158
  403.8 11.7 %copy-start.4 = (bf16[512,3072]{1,0:T(8,128)(2,1)S(1)}, bf16[512,3072]{1,0:T(8,128)(2,1)}, u32[]{:S(2)}) copy-start(bf16[512,3072]{1,0:T(8,128)(2,1)} %param.12) | copy-start | bytes 9437188
  415.5 3.1 copy-start.1
Sparse Core Ops, SparseCore 0:
  10.3 110.8 all-gather.2
  142.5 132.9 reduce-scatter.1
  277.9 99.8 all-gather.4
where the time goes:
time: 425 us
  waiting for transfers between devices  288 us (68%)
  matrix products  57.1 us (13%)
  blocking collectives  45.2 us (11%)
  other arithmetic  15.5 us (4%)
  between operations  13.8 us (3%)
  local copies, waits for them, and re-layouts  5.31 us (1%)
    reduce_scatter x1, waiting for transfers between devices, gathered_plan(): lax.psum_scatter(partial_value, GROUP, scatter_dimension=0, tiled=True)  133 us
    all_gather x1, waiting for transfers between devices, gathered_plan(): all_err = lax.all_gather(residual, GROUP, axis=0, tiled=True)  100 us
    all_gather x1, waiting for transfers between devices, gathered_plan(): all_x = lax.all_gather(activations, GROUP, axis=0, tiled=True)  54.2 us
    all_gather x1, blocking collectives, gathered_plan(): all_ids = lax.all_gather(ids, GROUP, axis=0, tiled=True)  45.2 us
    dot_general x1, matrix products, gathered_plan(): lax.dot_general(all_x, grad_pre, (((0,), (0,)), ((), ())), preferred_elem...  23.1 us
    dot_general x1, matrix products, gathered_plan(): lax.dot_general(code_vals, all_err, (((0,), (0,)), ((), ())), preferred_e...  11.7 us
    dot_general x1, matrix products, gathered_plan(): jnp.dot(all_x, enc_weight, preferred_element_type=jnp.float32) + enc_bias  10.1 us
    dot_general x1, matrix products, gathered_plan(): jnp.dot(code_vals, dec_weight, preferred_element_type=jnp.float32)  9.73 us
  transfers between devices with their start and end apart: 3, of which 3 were waited for; matrix products, arithmetic and copies ran while one was open for 3% of the time, Pallas kernels for 0%

commit v1 on v0

--- a/solution.py
+++ b/solution.py
@@ -155,7 +155,14 @@
     residual = (summed.astype(jnp.float32) + dec_bias - activations.astype(jnp.float32)).astype(
         jnp.bfloat16
     )
-    all_err = lax.all_gather(residual, GROUP, axis=0, tiled=True)
+    ways, here, turn = (lax.axis_size(GROUP), lax.axis_index(GROUP), residual.shape[0])
+    line, have = (residual, 1)
+    while have < ways:
+        line = jnp.concatenate(
+            [line, lax.ppermute(line, GROUP, [(d, (d - have) % ways) for d in range(ways)])], axis=0
+        )
+        have = 2 * have
+    all_err = jnp.roll(line, here * turn, axis=0)
     grad_codes = lax.dot_general(
         all_err, dec_weight, (((1,), (1,)), ((), ())), preferred_element_type=jnp.float32
     )

time: 425 us -> 625 us (1.47)
  waiting for transfers between devices: 288 us -> 438 us
  local copies, waits for them, and re-layouts: 5.31 us -> 28.9 us
  matrix products: 57.1 us -> 69.1 us
  other arithmetic: 15.5 us -> 22.7 us
  starting transfers between devices: 0.12 us -> 6.54 us
    ppermute x0 -> x4, waiting for transfers between devices: none -> 251 us  [gathered_plan(): lax.ppermute(line, GROUP, [(d, (d - have) % ways) for d in range(ways)])]
    all_gather x1 -> x0, waiting for transfers between devices: 100 us -> none  [gathered_plan(): all_err = lax.all_gather(residual, GROUP, axis=0, tiled=True)]
    unnamed x18 -> x40, local copies, waits for them, and re-layouts: 5.06 us -> 22.6 us
    dot_general x1, matrix products: 23.1 us -> 34.8 us  [gathered_plan(): lax.dot_general(all_x, grad_pre, (((0,), (0,)), ((), ())), preferred_elem...]
    ppermute x0 -> x4, starting transfers between devices: none -> 6.46 us  [gathered_plan(): lax.ppermute(line, GROUP, [(d, (d - have) % ways) for d in range(ways)])]
  transfers between devices with their start and end apart: 3 -> 6, of which waited for: 3 -> 6; matrix products, arithmetic and copies ran while one was open for 3% -> 3% of each run, Pallas kernels for 0% -> 0%
where the time goes in v1:
time: 625 us
  waiting for transfers between devices  438 us (70%)
  matrix products  69.1 us (11%)
  blocking collectives  45.2 us (7%)
  local copies, waits for them, and re-layouts  28.9 us (5%)
  other arithmetic  22.7 us (4%)
  between operations  14.1 us (2%)
  starting transfers between devices  6.54 us (1%)
    ppermute x4, waiting for transfers between devices, gathered_plan(): lax.ppermute(line, GROUP, [(d, (d - have) % ways) for d in range(ways)])  251 us
    reduce_scatter x1, waiting for transfers between devices, gathered_plan(): lax.psum_scatter(partial_value, GROUP, scatter_dimension=0, tiled=True)  133 us
    all_gather x1, waiting for transfers between devices, gathered_plan(): all_x = lax.all_gather(activations, GROUP, axis=0, tiled=True)  54.2 us
    all_gather x1, blocking collectives, gathered_plan(): all_ids = lax.all_gather(ids, GROUP, axis=0, tiled=True)  45.2 us
    dot_general x1, matrix products, gathered_plan(): lax.dot_general(all_x, grad_pre, (((0,), (0,)), ((), ())), preferred_elem...  34.8 us
    unnamed x40, local copies, waits for them, and re-layouts  22.6 us
  transfers between devices with their start and end apart: 6, of which 6 were waited for; matrix products, arithmetic and copies ran while one was open for 3% of the time, Pallas kernels for 0%

profile of v1, /device:TPU:0, one launch (start us, length us, event | category | flops | bytes accessed | tf_op | source)
XLA Modules:
  0.0 625.0 jit_solution(77615142418770893)
XLA Ops:
  8.0 0.9 copy.20
  10.0 45.2 %all_gather.6 = s32[2048,64]{0,1:T(8,128)S(1)} all-gather(s32[128,64]{0,1:T(8,128)S(1)} %fusion.19), channel_id=1, replica_groups=mesh['grp'=2,'tok'=4,'feat'=4] {'tok','feat'}, dimensions={0}, use_global_device_ids=true | all-gather | bytes 557056 | tf_op jit(solution)/shard_map/all_gather | solution.py:146
  55.6 8.9 %select_reduce_fusion = s32[2048,64]{0,1:T(8,128)S(1)} fusion(s32[2048,64]{0,1:T(8,128)S(1)} %get-tuple-element.19, s32[2048,64]{0,1:T(8,128)S(1)} %get-tuple-element.18), kind=kLoop, calls=%fused_computation | loop fusion | flops 25034752 | bytes 1572864 | tf_op jit(solution)/shard_map/reduce_sum | solution.py:130
  64.6 2.5 fusion.13
  67.0 54.2 %all-gather.2.cloned.1.call-done = bf16[2048,3072]{1,0:T(8,128)(2,1)} async-done(((bf16[128,3072]{1,0:T(8,128)(2,1)}), bf16[2048,3072]{1,0:T(8,128)(2,1)}) %all-gather.2.cloned.1.call-update) | async-done | bytes 12582928 | tf_op jit(solution)/shard_map/all_gather | solution.py:147
  121.2 10.1 %select_convert_fusion.1 = bf16[2048,512]{1,0:T(8,128)(2,1)S(1)} fusion(pred[2048,512]{1,0:T(32,128)(4,1)} %fusion.13, bf16[2048,3072]{1,0:T(8,128)(2,1)} %all-gather.2.cloned.1.call-done, bf16[3072,512]{1,0:T(8,128)(2,1)S(1)} %copy-done, f32[512]{0:T(512)S(1)} %copy-done.12), kind=kOutput, calls=%fused_computation.17 | convolution fusion | flops 6445596672 | bytes 18876416 | tf_op jit(solution)/shard_map/dot_general | solution.py:149
  131.3 1.3 copy-done.13
  132.7 9.7 %convolution_convert_fusion = bf16[2048,3072]{1,0:T(8,128)(2,1)} fusion(bf16[2048,512]{1,0:T(8,128)(2,1)S(1)} %select_convert_fusion.1, bf16[512,3072]{1,0:T(8,128)(2,1)S(1)} %copy-done.9), kind=kOutput, calls=%fused_computation.2 | convolution fusion | flops 6448742400 | bytes 17825792 | tf_op jit(solution)/shard_map/dot_general | solution.py:151
  142.3 133.0 %reduce-scatter.2.cloned.1.call-done = bf16[128,3072]{1,0:T(8,128)(2,1)} async-done(((bf16[2048,3072]{1,0:T(8,128)(2,1)}), bf16[128,3072]{1,0:T(8,128)(2,1)}) %reduce-scatter.2.cloned.1.call-update) | async-done | bytes 786448 | tf_op jit(solution)/shard_map/reduce_scatter | solution.py:154
  275.3 2.3 constant_dynamic-update-slice_fusion.9
  277.6 2.1 collective-permute-start
  279.7 16.8 %collective-permute-done = bf16[128,3072]{1,0:T(8,128)(2,1)S(1)} collective-permute-done((bf16[128,3072]{1,0:T(8,128)(2,1)S(1)}, bf16[128,3072]{1,0:T(8,128)(2,1)S(1)}, u32[]{:S(2)}, u32[]{:S(2)}) %collective-permute-start) | collective-permute-done | bytes 786464 | tf_op jit(solution)/shard_map/ppermute | solution.py:162
  296.6 1.6 collective-permute-start.1
  298.2 68.3 %collective-permute-done.1 = bf16[256,3072]{1,0:T(8,128)(2,1)S(1)} collective-permute-done((bf16[256,3072]{1,0:T(8,128)(2,1)S(1)}, bf16[256,3072]{1,0:T(8,128)(2,1)S(1)}, u32[]{:S(2)}, u32[]{:S(2)}) %collective-permute-start.1) | collective-permute-done | bytes 1572896 | tf_op jit(solution)/shard_map/ppermute | solution.py:162
  366.7 1.6 collective-permute-start.2
  368.3 34.8 %collective-permute-done.2 = bf16[512,3072]{1,0:T(8,128)(2,1)S(1)} collective-permute-done((bf16[512,3072]{1,0:T(8,128)(2,1)S(1)}, bf16[512,3072]{1,0:T(8,128)(2,1)S(1)}, u32[]{:S(2)}, u32[]{:S(2)}) %collective-permute-start.2) | collective-permute-done | bytes 3145760 | tf_op jit(solution)/shard_map/ppermute | solution.py:162
  403.1 3.1 pad_maximum_fusion
  406.2 1.2 collective-permute-start.3
  407.4 2.1 constant_dynamic-update-slice_fusion.8
  409.4 2.7 constant_dynamic-update-slice_fusion.7
  412.1 1.9 constant_dynamic-update-slice_fusion.6
  414.0 130.6 %collective-permute-done.3 = bf16[1024,3072]{1,0:T(8,128)(2,1)} collective-permute-done((bf16[1024,3072]{1,0:T(8,128)(2,1)}, bf16[1024,3072]{1,0:T(8,128)(2,1)}, u32[]{:S(2)}, u32[]{:S(2)}) %collective-permute-start.3) | collective-permute-done | bytes 6291488 | tf_op jit(solution)/shard_map/ppermute | solution.py:162
  544.6 5.9 constant_dynamic-update-slice_fusion.5
  550.5 1.0 constant_dynamic-update-slice_fusion.4
  551.5 0.9 constant_dynamic-update-slice_fusion.3
  552.4 1.3 constant_dynamic-update-slice_fusion.2
  553.7 1.9 constant_dynamic-update-slice_fusion.1
  555.5 6.0 constant_dynamic-update-slice_fusion
  561.5 12.1 %fusion.5 = (f32[512]{0:T(512)S(1)}, f32[512]{0:T(512)S(1)}, f32[512,3072]{1,0:T(8,128)}) fusion(bf16[512,3072]{1,0:T(8,128)(2,1)S(1)} %copy-done.10, bf16[2048,512]{1,0:T(8,128)(2,1)S(1)} %copy-done.14, bf16[4096,3072]{1,0:T(8,128)(2,1)} %constant_dynamic-update-slice_fusion, s32[]{:T(128)S(6)} %select_n.78), kind=kOutput, calls=%fused_computation.11 | convolution fusion | flops 6450314240 | bytes 24121348 | tf_op jit(solution)/shard_map/dot_general | solution.py:173
  573.6 34.8 %fusion.8 = bf16[3072,512]{0,1:T(8,128)(2,1)S(1)} fusion(bf16[2048,3072]{1,0:T(8,128)(2,1)} %all-gather.2.cloned.1.call-done, pred[2048,512]{1,0:T(32,128)(4,1)} %fusion.13, bf16[512,3072]{1,0:T(8,128)(2,1)} %param.12, bf16[4096,3072]{1,0:T(8,128)(2,1)} %constant_dynamic-update-slice_fusion, s32[]{:T(128)S(6)} %select_n.78), kind=kOutput, calls=%fused_computation.19 | convolution fusion | flops 12888571904 | bytes 32505860 | tf_op jit(solution)/shard_map/dot_general | solution.py:170
  608.4 2.8 copy.21
  611.2 6.9 %fusion.7 = bf16[512,3072]{1,0:T(8,128)(2,1)} fusion(f32[512,3072]{1,0:T(8,128)} %get-tuple-element.20, bf16[512,3072]{1,0:T(8,128)(2,1)} %param.12, f32[512]{0:T(512)S(1)} %add_divide_fusion), kind=kLoop, calls=%fused_computation.13 | loop fusion | flops 6291456 | bytes 12584960 | tf_op jit(solution)/shard_map/convert_element_type | solution.py:180
  (41 shorter events, 2.6 us)
Async XLA Ops:
  7.2 114.0 %copy-start = (bf16[3072,512]{1,0:T(8,128)(2,1)S(1)}, bf16[3072,512]{1,0:T(8,128)(2,1)}, u32[]{:S(2)}) copy-start(bf16[3072,512]{1,0:T(8,128)(2,1)} %param.10) | copy-start | bytes 9437188
  7.2 114.0 %all-gather.2.cloned.1.call-start = ((), (), s32[]{:S(2)}) async-start(), calls=%async_computation.1 | async-start | bytes 13369344 | tf_op jit(solution)/shard_map/all_gather | solution.py:147
  7.9 267.4 %reduce-scatter.2.cloned.1.call-start = ((), (), s32[]{:S(2)}) async-start(), calls=%async_computation.2 | async-start | bytes 13369344 | tf_op jit(solution)/shard_map/reduce_scatter | solution.py:154
  55.6 65.6 %copy-start.12 = (f32[512]{0:T(512)S(1)}, f32[512]{0:T(512)}, u32[]{:S(2)}) copy-start(f32[512]{0:T(512)} %param.11) | copy-start | bytes 6148
  121.2 11.5 %copy-start.9 = (bf16[512,3072]{1,0:T(8,128)(2,1)S(1)}, bf16[512,3072]{1,0:T(8,128)(2,1)}, u32[]{:S(2)}) copy-start(bf16[512,3072]{1,0:T(8,128)(2,1)} %param.12) | copy-start | bytes 9437188
  131.3 1.3 copy-start.13
  142.3 133.0 %copy-start.8 = (bf16[128,3072]{1,0:T(8,128)(2,1)S(1)}, bf16[128,3072]{1,0:T(8,128)(2,1)}, u32[]{:S(2)}) copy-start(bf16[128,3072]{1,0:T(8,128)(2,1)} %param.7) | copy-start | bytes 2359300
  142.3 133.0 %copy-start.11 = (f32[3072]{0:T(1024)S(1)}, f32[3072]{0:T(1024)}, u32[]{:S(2)}) copy-start(f32[3072]{0:T(1024)} %param.13) | copy-start | bytes 36868
  277.6 128.6 %copy-start.4 = (bf16[128,3072]{1,0:T(8,128)(2,1)}, bf16[128,3072]{1,0:T(8,128)(2,1)S(1)}, u32[]{:S(2)}) copy-start(bf16[128,3072]{1,0:T(8,128)(2,1)S(1)} %get-tuple-element.17) | copy-start | bytes 2359300
  277.6 18.9 %collective-permute-start = (bf16[128,3072]{1,0:T(8,128)(2,1)S(1)}, bf16[128,3072]{1,0:T(8,128)(2,1)S(1)}, u32[]{:S(2)}, u32[]{:S(2)}) collective-permute-start(bf16[128,3072]{1,0:T(8,128)(2,1)S(1)} %get-tuple-element.17), channel_id=1, source_target_pairs={{0,15},{1,0},{2,1},{3,2},{4,3},{5,4},{6,5},{7,6},{8,7},{9,8},{10,9... | collective-permute-start | bytes 2359304 | tf_op jit(solution)/shard_map/ppermute | solution.py:162
  296.5 109.7 %copy-start.6 = (bf16[128,3072]{1,0:T(8,128)(2,1)}, bf16[128,3072]{1,0:T(8,128)(2,1)S(1)}, u32[]{:S(2)}) copy-start(bf16[128,3072]{1,0:T(8,128)(2,1)S(1)} %collective-permute-done) | copy-start | bytes 2359300
  296.6 69.9 %collective-permute-start.1 = (bf16[256,3072]{1,0:T(8,128)(2,1)S(1)}, bf16[256,3072]{1,0:T(8,128)(2,1)S(1)}, u32[]{:S(2)}, u32[]{:S(2)}) collective-permute-start(bf16[256,3072]{1,0:T(8,128)(2,1)S(1)} %pad_maximum_fusion.2), channel_id=1, source_target_pairs={{0,14},{1,15},{2,0},{3,1},{4,2},{5,3},{6,4},{7,5},{8,6},{9,7},{10,... | collective-permute-start | bytes 4718600 | tf_op jit(solution)/shard_map/ppermute | solution.py:162
  366.5 39.7 %copy-start.2 = (bf16[256,3072]{1,0:T(8,128)(2,1)}, bf16[256,3072]{1,0:T(8,128)(2,1)S(1)}, u32[]{:S(2)}) copy-start(bf16[256,3072]{1,0:T(8,128)(2,1)S(1)} %collective-permute-done.1) | copy-start | bytes 4718596
  366.7 36.4 %collective-permute-start.2 = (bf16[512,3072]{1,0:T(8,128)(2,1)S(1)}, bf16[512,3072]{1,0:T(8,128)(2,1)S(1)}, u32[]{:S(2)}, u32[]{:S(2)}) collective-permute-start(bf16[512,3072]{1,0:T(8,128)(2,1)S(1)} %pad_maximum_fusion.1), channel_id=1, source_target_pairs={{0,12},{1,13},{2,14},{3,15},{4,0},{5,1},{6,2},{7,3},{8,4},{9,5},{1... | collective-permute-start | bytes 9437192 | tf_op jit(solution)/shard_map/ppermute | solution.py:162
  406.2 138.4 %collective-permute-start.3 = (bf16[1024,3072]{1,0:T(8,128)(2,1)}, bf16[1024,3072]{1,0:T(8,128)(2,1)}, u32[]{:S(2)}, u32[]{:S(2)}) collective-permute-start(bf16[1024,3072]{1,0:T(8,128)(2,1)} %pad_maximum_fusion), channel_id=1, source_target_pairs={{0,8},{1,9},{2,10},{3,11},{4,12},{5,13},{6,14},{7,15},{8,0},{9,1},... | collective-permute-start | bytes 18874376 | tf_op jit(solution)/shard_map/ppermute | solution.py:162
  414.0 136.5 %copy-start.5 = (bf16[128,3072]{1,0:T(8,128)(2,1)S(1)}, bf16[128,3072]{1,0:T(8,128)(2,1)}, u32[]{:S(2)}) copy-start(bf16[128,3072]{1,0:T(8,128)(2,1)} %copy-done.4) | copy-start | bytes 2359300
  414.0 137.5 %copy-start.7 = (bf16[128,3072]{1,0:T(8,128)(2,1)S(1)}, bf16[128,3072]{1,0:T(8,128)(2,1)}, u32[]{:S(2)}) copy-start(bf16[128,3072]{1,0:T(8,128)(2,1)} %copy-done.6) | copy-start | bytes 2359300
  414.0 138.4 %copy-start.3 = (bf16[256,3072]{1,0:T(8,128)(2,1)S(1)}, bf16[256,3072]{1,0:T(8,128)(2,1)}, u32[]{:S(2)}) copy-start(bf16[256,3072]{1,0:T(8,128)(2,1)} %copy-done.2) | copy-start | bytes 4718596
  555.5 6.0 copy-start.10
  555.5 6.0 copy-start.14
  611.2 6.9 %copy-start.1 = (bf16[3072,512]{1,0:T(8,128)(2,1)S(1)}, bf16[3072,512]{1,0:T(8,128)(2,1)}, u32[]{:S(2)}) copy-start(bf16[3072,512]{1,0:T(8,128)(2,1)} %param.10) | copy-start | bytes 9437188
Sparse Core Ops, SparseCore 0:
  10.3 110.8 all-gather.1
  142.5 132.7 reduce-scatter.1
